TPU v7x, 32 devices: a whole 2x2x4 slice. The times are simulated.
32 devices in a mesh: video: 2 (over y), rows: 4 (over z), cols: 4 (over x, core).
Axes of the slice: x: 2, y: 2, z: 4, core: 2. Of those that a mesh axis runs over, the one named last changes fastest.
Arguments:
- frame_in: bfloat16 [64, 80, 512], P(('video', 'rows'), 'cols'), parts along dimension 0, may hold values from -6 to 6
- norm_gain: float32 [512], replicated, may hold values from 0.5 to 1.5
- w_query: bfloat16 [512, 512], replicated, may hold values from -2 to 2
- w_key: bfloat16 [512, 512], replicated, may hold values from -0.125 to 0.125
- w_value: bfloat16 [512, 512], replicated, may hold values from -0.25 to 0.25
- w_out: bfloat16 [512, 512], replicated, may hold values from -0.25 to 0.25
- conv_gain: float32 [512], replicated, may hold values from 0.5 to 1.5
- conv_cache: bfloat16 [2, 64, 80, 512], P(None, ('video', 'rows'), 'cols'), parts along dimension 1, may hold values from -6 to 6
- w_conv: bfloat16 [3, 3, 3, 512, 256], replicated, may hold values from -0.0546875 to 0.0546875
- conv_bias: float32 [256], replicated, may hold values from -0.5 to 0.5
Outputs:
- hidden: bfloat16 [64, 80, 512], P(('video', 'rows'), 'cols'), parts along dimension 0
- mixed_out: bfloat16 [64, 80, 256], P(('video', 'rows'), 'cols'), parts along dimension 0
There are 2 independent parts, one for each index of `video`. A program takes and returns all parts, laid end to end along the dimension named above; an argument that names none is the same for every part. Nothing has to cross between parts.
All inputs are finite; a program needn't handle non-finite values.
Results may differ from a plain program's by a relative error of at most 0.012.
Values may be sent and summed in bfloat16 or wider, within the bound.
No kernel may reach another device: no remote copies, remote signals or barrier semaphores. Data moves between devices by JAX's collectives and lax.ppermute only.
A program may use at most 128 MiB of HBM per device.

v0:
```python
import functools
import math

import jax
import jax.numpy as jnp
from jax import lax
from jax.experimental import pallas as pl
from jax.experimental.pallas import tpu as pltpu
from jax.sharding import PartitionSpec as P


EPS = 1e-06
AXES = ("rows", "cols")
F32 = jnp.float32
BF16 = jnp.bfloat16
VM = pl.BlockSpec(memory_space=pltpu.VMEM)


def near(value):
    return pltpu.with_memory_space_constraint(value, pltpu.VMEM)


def call(kernel, outs, args, limit=16 << 20, far_args=(), far=False, scratch=()):
    return pl.pallas_call(
        kernel,
        in_specs=[VM] * len(args) + [pl.BlockSpec(memory_space=pltpu.HBM)] * len(far_args),
        out_specs=[VM] * len(outs),
        out_shape=[
            jax.ShapeDtypeStruct(shape, dtype) if far else pltpu.VMEM(shape, dtype)
            for shape, dtype in outs
        ],
        scratch_shapes=scratch,
        compiler_params=pltpu.CompilerParams(vmem_limit_bytes=limit),
    )(*[near(a) for a in args], *[pltpu.with_memory_space_constraint(a, pltpu.HBM) for a in far_args])


def chip_cycle(height, width):
    if width == 1 or height == 1:
        return [(z, x) for z in range(height) for x in range(width)]
    order = []
    for x in range(width):
        inner = range(1, height) if x % 2 == 0 else range(height - 1, 0, -1)
        order += [(z, x) for z in inner]
    return order + [(0, x) for x in range(width - 1, -1, -1)]


def permutations(rows, cols):
    def at(z, x, core):
        return z * cols + 2 * x + core

    walk = chip_cycle(rows, cols // 2)
    ring = []
    for k, here in enumerate(walk):
        there = walk[(k + 1) % len(walk)]
        ring += [(at(*here, 0), at(*there, 0)), (at(*there, 1), at(*here, 1))]
    twin = [(i, i ^ 1) for i in range(rows * cols)]
    down = [(i, i + cols) for i in range((rows - 1) * cols)]
    up = [(j, i) for i, j in down]
    cross = []
    for r in range(rows):
        for c in range(1, cols - 1, 2):
            i = r * cols + c
            cross += [(i, i + 1), (i + 1, i)]
    return len(walk), ring, twin, down, up, cross


def edge_slots(width):
    return -(-(width + 2) // 16) * 16


def edge_rows(width):
    return -(-width // 8) * 8


def side_slots(height):
    return height + 8


def rms_scaled(values, gain):
    mean_sq = jnp.mean(values * values, axis=-1, keepdims=True)
    return values * lax.rsqrt(mean_sq + EPS) * gain


def dot(a, b):
    return jnp.dot(a, b, preferred_element_type=F32)


def dot_t(a, b):
    return lax.dot_general(a, b, (((1,), (1,)), ((), ())), preferred_element_type=F32)


def row_edge(tile, r):
    width, _, channels = tile.shape
    fill = jnp.zeros((edge_rows(width) - width, channels), F32)
    return jnp.concatenate([tile[c, r : r + 1, :] for c in range(width)] + [fill], axis=0)


def load_tiles(frame_hbm, cache_hbm, gain_hbm, frame_ref, cache_ref, gain_ref, sems):
    copies = [
        pltpu.make_async_copy(frame_hbm, frame_ref, sems.at[0]),
        pltpu.make_async_copy(cache_hbm, cache_ref, sems.at[1]),
        pltpu.make_async_copy(gain_hbm, gain_ref, sems.at[2]),
    ]
    for copy in copies:
        copy.start()
    for copy in copies:
        copy.wait()


def pack_rows_kernel(frame_hbm, cache_hbm, gain_hbm, frame_ref, cache_ref, gain_ref, first_ref, last_ref, sems):
    load_tiles(frame_hbm, cache_hbm, gain_hbm, frame_ref, cache_ref, gain_ref, sems)
    height = frame_ref.shape[1]
    for t in range(3):
        tile = (frame_ref[...] if t == 2 else cache_ref[t]).astype(F32)
        first_ref[t] = row_edge(tile, 0).astype(BF16)
        last_ref[t] = row_edge(tile, height - 1).astype(BF16)


def faces_up():
    col = lax.axis_index("cols")
    return lax.rem(lax.rem(col, 2) + lax.div(col, 2), 2)


def pack_swap_kernel(frame_hbm, cache_hbm, gain_hbm, frame_ref, cache_ref, gain_ref, edge_ref, swap_ref, sems):
    load_tiles(frame_hbm, cache_hbm, gain_hbm, frame_ref, cache_ref, gain_ref, sems)
    width, height, channels = frame_ref.shape
    count, rows = width * height, edge_rows(width)
    up = faces_up()
    odd = lax.rem(lax.axis_index("cols"), 2)
    swap_ref[:count] = frame_ref[...].reshape(count, channels)
    for t in range(2):
        tile = cache_ref[t].astype(F32)
        first, last = row_edge(tile, 0), row_edge(tile, height - 1)
        edge_ref[t * rows : (t + 1) * rows] = jnp.where(up == 1, first, last).astype(BF16)
        at = count + t * rows
        swap_ref[at : at + rows] = jnp.where(up == 1, last, first).astype(BF16)
        at = count + 2 * rows + t * height
        swap_ref[at : at + height] = jnp.where(odd == 1, tile[0], tile[width - 1]).astype(BF16)


def join_edges_kernel(frame_ref, edge_ref, partner_ref, out_ref):
    width, height, channels = frame_ref.shape
    count, rows = width * height, edge_ref.shape[0]
    out_ref[:count] = frame_ref[...].reshape(count, channels)
    out_ref[count : 2 * count] = partner_ref[:count]
    out_ref[2 * count : 2 * count + rows] = edge_ref[...]
    out_ref[2 * count + rows :] = partner_ref[count : count + rows]


def split_kernel(height, arrived_ref, chain_ref, edges_ref):
    count = chain_ref.shape[0] // 2
    width = count // height
    rows = edge_rows(width)
    up = faces_up()
    chain_ref[...] = arrived_ref[: 2 * count]
    for k in range(2):
        to = k * 3 * rows
        at = 2 * count + k * 2 * rows
        edges_ref[to : to + 2 * rows] = arrived_ref[at : at + 2 * rows]
        tile = arrived_ref[k * count : (k + 1) * count].astype(F32).reshape(width, height, -1)
        edge = jnp.where(up == 1, row_edge(tile, 0), row_edge(tile, height - 1))
        edges_ref[to + 2 * rows : to + 3 * rows] = edge.astype(BF16)


def sort_edges_kernel(
    frame_ref, cache_ref, partner_ref, mine_ref, theirs_ref, top_ref, bottom_ref, twin_ref, cross_ref
):
    width, height, channels = frame_ref.shape
    count, rows = width * height, top_ref.shape[1]
    up = faces_up()
    odd = lax.rem(lax.axis_index("cols"), 2)
    row = lax.axis_index("rows")
    has_top, has_bottom = row > 0, row < lax.axis_size("rows") - 1
    fill = jnp.zeros((side_slots(height) - height - 2, channels), F32)
    for t in range(3):
        pair = []
        for k in range(2):
            mine = mine_ref[(3 * k + t) * rows : (3 * k + t + 1) * rows].astype(F32)
            theirs = theirs_ref[(3 - 3 * k + t) * rows : (4 - 3 * k + t) * rows].astype(F32)
            top = jnp.where(has_top, jnp.where(up == 1, theirs, mine), 0.0)
            bottom = jnp.where(has_bottom, jnp.where(up == 1, mine, theirs), 0.0)
            pair.append((top, bottom))
        (top, bottom), (twin_top, twin_bottom) = pair
        top_ref[t] = top.astype(BF16)
        bottom_ref[t] = bottom.astype(BF16)

        def facing(first, value, axis_rows):
            a, b = value[axis_rows(0)], value[axis_rows(width - 1)]
            return jnp.where(first, a, b)

        if t == 2:
            block = partner_ref[:count].astype(F32)
            column = facing(odd == 0, block, lambda c: slice(c * height, (c + 1) * height))
        else:
            at = count + 2 * rows + t * height
            column = partner_ref[at : at + height].astype(F32)
        corners = [facing(odd == 0, v, lambda c: slice(c, c + 1)) for v in (twin_top, twin_bottom)]
        twin_ref[t] = jnp.concatenate([column, *corners, fill], axis=0).astype(BF16)
        tile = (frame_ref[...] if t == 2 else cache_ref[t]).astype(F32)
        column = jnp.where(odd == 0, tile[0], tile[width - 1])
        corners = [facing(odd == 0, v, lambda c: slice(c, c + 1)) for v in (top, bottom)]
        cross_ref[t] = jnp.concatenate([column, *corners, fill], axis=0).astype(BF16)


def pack_cols_kernel(frame_ref, cache_ref, top_ref, bottom_ref, twin_ref, cross_ref):
    width, height, channels = frame_ref.shape
    odd = lax.rem(lax.axis_index("cols"), 2)
    fill = jnp.zeros((side_slots(height) - height - 2, channels), F32)
    for t in range(3):
        sides = []
        for c in (0, width - 1):
            own = (frame_ref[c] if t == 2 else cache_ref[t, c]).astype(F32)
            top = top_ref[t].astype(F32)[c : c + 1, :]
            bottom = bottom_ref[t].astype(F32)[c : c + 1, :]
            sides.append(jnp.concatenate([own, top, bottom, fill], axis=0))
        left, right = sides
        twin_ref[t] = jnp.where(odd == 1, left, right).astype(BF16)
        cross_ref[t] = jnp.where(odd == 1, right, left).astype(BF16)


def extended(own, top, bottom, twin, cross, odd):
    height = twin.shape[0] - side_slots(0)
    left = jnp.where(odd == 1, twin, cross)
    right = jnp.where(odd == 1, cross, twin)
    width = own.shape[0] // height
    slots = edge_slots(width)
    slot = lax.broadcasted_iota(jnp.int32, (slots, own.shape[1]), 0)
    fill = jnp.zeros((slots - top.shape[0], own.shape[1]), F32)

    def edge(row, k):
        row = jnp.concatenate([row, fill], axis=0)
        row = jnp.where(slot == width, right[k : k + 1, :], row)
        return jnp.where(slot == slots - 1, left[k : k + 1, :], row)

    return jnp.concatenate(
        [edge(top, height), left[:height], own, right[:height], edge(bottom, height + 1)], axis=0
    )


def conv_rows(ext_len, slots, i):
    return (0 if i == 0 else slots), (ext_len if i == 2 else ext_len - slots)


def add_taps(sums, products, i, j, height, count):
    slots = edge_slots(count // height)
    main = products[slots:] if i == 0 else products
    part = main[j * height : j * height + count]
    edge = None
    if i == 0:
        edge = products[:slots]
    if i == 2:
        edge = products[products.shape[0] - slots :]
    if edge is not None and j != 1:
        edge = pltpu.roll(edge, 1 if j == 0 else slots - 1, 0)
    if sums is None:
        return part, edge
    return sums[0] + part, (None if edge is None else sums[1] + edge)


def shifted_rows(sums, i, height):
    main, edge = sums
    if i == 1:
        return main
    count, out = main.shape
    width = count // height
    tile = main.reshape(width, height, out)
    moved = pltpu.roll(tile, 1 if i == 0 else height - 1, 1)
    row = lax.broadcasted_iota(jnp.int32, (height, out), 0)
    at = 0 if i == 0 else height - 1
    cells = [jnp.where(row == at, edge[c : c + 1, :], moved[c]) for c in range(width)]
    return jnp.concatenate(cells, axis=0)


def cache_conv_kernel(cache_ref, top_ref, bottom_ref, twin_ref, cross_ref, w_ref, out_ref):
    width, height, channels = cache_ref.shape[1:]
    count = width * height
    odd = lax.rem(lax.axis_index("cols"), 2)
    exts = [
        extended(
            cache_ref[t].reshape(count, channels).astype(F32),
            top_ref[t].astype(F32),
            bottom_ref[t].astype(F32),
            twin_ref[t].astype(F32),
            cross_ref[t].astype(F32),
            odd,
        ).astype(BF16)
        for t in range(2)
    ]
    result = None
    for i in range(3):
        lo, hi = conv_rows(exts[0].shape[0], edge_slots(width), i)
        sums = None
        for j in range(3):
            products = dot(exts[0][lo:hi], w_ref[0, i, j]) + dot(exts[1][lo:hi], w_ref[1, i, j])
            sums = add_taps(sums, products, i, j, height, count)
        value = shifted_rows(sums, i, height)
        result = value if result is None else result + value
    out_ref[...] = result


def query_kernel(
    frame_ref, top_ref, bottom_ref, twin_ref, cross_ref, gain_ref, wq_ref, wk_ref, raw_ref, keys_ref
):
    width, height, channels = frame_ref.shape
    odd = lax.rem(lax.axis_index("cols"), 2)
    tokens = extended(
        frame_ref[...].reshape(width * height, channels).astype(F32),
        top_ref[2].astype(F32),
        bottom_ref[2].astype(F32),
        twin_ref[2].astype(F32),
        cross_ref[2].astype(F32),
        odd,
    )
    raw_ref[...] = tokens.astype(BF16)
    normed = rms_scaled(tokens, gain_ref[...]).astype(BF16)
    rows = (dot(normed, wq_ref[...]) * (1.0 / math.sqrt(channels))).astype(BF16)
    keys_ref[...] = dot_t(rows, wk_ref[...]).astype(BF16)


def lanes(value, width):
    return jnp.broadcast_to(value, (value.shape[0], width))


def key_rows(refs, gain):
    parts = [
        rms_scaled(ref[...].reshape(-1, gain.shape[1]).astype(F32), gain).astype(BF16) for ref in refs
    ]
    return parts[0] if len(parts) == 1 else jnp.concatenate(parts, axis=0)


def fold_kernel(blocks, first, gain_ref, own_ref, twin_ref, *refs):
    keys = key_rows(refs[:blocks], gain_ref[...])
    states, outs = ((None, None), refs[blocks:]) if first else (refs[blocks:-2], refs[-2:])
    channels = keys.shape[1]
    length = own_ref.shape[0]
    all_scores = dot_t(jnp.concatenate([own_ref[...], twin_ref[...]], axis=0), keys)
    peaks, totals, weights = [], [], []
    for k, state in enumerate(states):
        scores = all_scores[k * length : (k + 1) * length]
        peak = jnp.max(scores, axis=1, keepdims=True)
        if not first:
            peak = jnp.maximum(peak, state[:, channels : channels + 1])
        part = jnp.exp(scores - peak)
        peaks.append(peak)
        totals.append(jnp.sum(part, axis=1, keepdims=True))
        weights.append(part.astype(BF16))
    all_summed = dot(jnp.concatenate(weights, axis=0), keys)
    for k, (state, out) in enumerate(zip(states, outs)):
        summed, total, peak = all_summed[k * length : (k + 1) * length], totals[k], peaks[k]
        if not first:
            fade = jnp.exp(state[:, channels : channels + 1] - peak)
            total = total + fade * state[:, channels + 128 : channels + 129]
            summed = summed + fade * state[:, :channels]
        out[:, :channels] = summed
        out[:, channels : channels + 128] = lanes(peak, 128)
        out[:, channels + 128 :] = lanes(total, 128)


def fold(states, own, twin, gain, blocks):
    length, channels = own.shape
    shape = ((length, channels + 256), F32)
    first = states is None
    args = (gain, own, twin, *blocks, *(() if first else states))
    return call(functools.partial(fold_kernel, len(blocks), first), [shape, shape], args, 24 << 20)


def fetch_kernel(*refs):
    sems = refs[-1]
    sources, targets = refs[: len(refs) // 2], refs[len(refs) // 2 : -1]
    copies = [
        pltpu.make_async_copy(source, target, sems.at[k])
        for k, (source, target) in enumerate(zip(sources, targets))
    ]
    for copy in copies:
        copy.start()
    for copy in copies:
        copy.wait()


def finish_kernel(
    height, state_ref, other_ref, query_ref, last_ref, key_gain_ref, raw_ref, partial_ref,
    wv_ref, wo_ref, gain_ref, bias_ref, w_ref, hidden_ref, mixed_ref,
):
    length, channels = raw_ref.shape
    count, out = partial_ref.shape
    slots = edge_slots(count // height)
    row = lax.axis_index("rows")
    col = lax.axis_index("cols")
    has_top, has_bottom = row > 0, row < lax.axis_size("rows") - 1
    has_left, has_right = col > 0, col < lax.axis_size("cols") - 1

    keys = key_rows((last_ref,), key_gain_ref[...])
    scores = dot_t(query_ref[...], keys)
    peak_a, peak_b = state_ref[:, channels : channels + 1], other_ref[:, channels : channels + 1]
    peak = jnp.maximum(jnp.maximum(peak_a, peak_b), jnp.max(scores, axis=1, keepdims=True))
    fade_a, fade_b = jnp.exp(peak_a - peak), jnp.exp(peak_b - peak)
    weights = jnp.exp(scores - peak)
    total = jnp.sum(weights, axis=1, keepdims=True)
    total = total + fade_a * state_ref[:, channels + 128 : channels + 129]
    total = total + fade_b * other_ref[:, channels + 128 : channels + 129]
    summed = dot(weights.astype(BF16), keys)
    summed = summed + fade_a * state_ref[:, :channels] + fade_b * other_ref[:, :channels]
    pooled = (summed / total).astype(BF16)
    attended = dot(pooled, wv_ref[...]).astype(BF16)
    hidden = (raw_ref[...].astype(F32) + dot(attended, wo_ref[...])).astype(BF16)
    wide = hidden.astype(F32)
    value = rms_scaled(wide, gain_ref[...])
    value = value / (1.0 + jnp.exp(-value))
    slot = lax.broadcasted_iota(jnp.int32, (length, 1), 0)
    main_end = length - slots
    width = count // height
    in_top, in_bottom = slot < slots, slot >= main_end
    in_left = (slot >= slots) & (slot < slots + height)
    in_right = (slot >= main_end - height) & (slot < main_end)
    in_left = in_left | (slot == slots - 1) | (slot == length - 1)
    in_right = in_right | (slot == width) | (slot == main_end + width)
    outside = (in_top & jnp.logical_not(has_top)) | (in_bottom & jnp.logical_not(has_bottom))
    outside = outside | (in_left & jnp.logical_not(has_left)) | (in_right & jnp.logical_not(has_right))
    ext = jnp.where(outside, 0.0, value).astype(BF16)

    own = hidden[slots + height : slots + height + count]
    hidden_ref[...] = own
    result = partial_ref[...] + own[:, :out].astype(F32) + bias_ref[...]
    for i in range(3):
        lo, hi = conv_rows(length, slots, i)
        sums = None
        for j in range(3):
            sums = add_taps(sums, dot(ext[lo:hi], w_ref[2, i, j]), i, j, height, count)
        result = result + shifted_rows(sums, i, height)
    mixed_ref[...] = result.astype(BF16)


def join_kernel(a_ref, b_ref, out_ref):
    count = b_ref.shape[0]
    out_ref[:count] = a_ref[...].reshape(b_ref.shape)
    out_ref[count:] = b_ref[...]


def narrow(cols):
    return cols == 4


def moved(value, pairs):
    return lax.ppermute(value, AXES, pairs)


def block(
    frame_in, norm_gain, w_query, w_key, w_value, w_out, conv_gain, conv_cache, w_conv, conv_bias
):
    height, width, channels = frame_in.shape
    out_channels = w_conv.shape[4]
    count = height * width
    chips, ring, twin_pairs, down, up, cross_pairs = permutations(
        lax.axis_size("rows"), lax.axis_size("cols")
    )
    frame_far = jnp.transpose(frame_in, (1, 0, 2))
    cache_far = jnp.transpose(conv_cache, (0, 2, 1, 3))
    gain_far = norm_gain.reshape(1, channels)

    rows = edge_rows(width)
    tiles = [(frame_far.shape, BF16), (cache_far.shape, BF16), (gain_far.shape, F32)]
    far_tiles = (frame_far, cache_far, gain_far)
    edge = ((3, rows, channels), BF16)
    side = ((3, side_slots(height), channels), BF16)
    pair = ((2 * count, channels), BF16)
    sems = [pltpu.SemaphoreType.DMA((3,))]
    hops = (chips - 1) // 2
    if narrow(lax.axis_size("cols")):
        frame, cache, gain, edges, to_partner = call(
            pack_swap_kernel,
            tiles + [((2 * rows, channels), BF16), ((count + 2 * (rows + height), channels), BF16)],
            (), far_args=far_tiles, scratch=sems,
        )
        partner = moved(to_partner, twin_pairs)
        (first_hop,) = call(join_edges_kernel, [((2 * count + 4 * rows, channels), BF16)], (frame, edges, partner))
        arrived = moved(first_hop, ring)
        chain, mine = call(functools.partial(split_kernel, height), [pair, ((6 * rows, channels), BF16)], (arrived,))
        theirs = moved(mine, twin_pairs)
        top, bottom, twin, to_cross = call(
            sort_edges_kernel, [edge, edge, side, side], (frame, cache, partner, mine, theirs)
        )
    else:
        frame, cache, gain, first_rows, last_rows = call(
            pack_rows_kernel, tiles + [edge, edge], (), far_args=far_tiles, scratch=sems
        )
        partner = moved(frame_far.reshape(count, channels), twin_pairs)
        (chain,) = call(join_kernel, [pair], (frame, partner))
        chain = moved(chain, ring)
        top = moved(last_rows, down)
        bottom = moved(first_rows, up)
        to_twin, to_cross = call(pack_cols_kernel, [side, side], (frame, cache, top, bottom))
        twin = moved(to_twin, twin_pairs)
    cross = moved(to_cross, cross_pairs)
    blocks = [frame, chain]
    for _ in range(1, hops):
        chain = moved(chain, ring)
        blocks.append(chain)
    last = moved(chain, ring)

    far_args = (
        w_query, w_key, w_value, w_out, conv_gain.reshape(1, channels),
        conv_bias.reshape(1, out_channels), w_conv,
    )
    w_query, w_key, w_value, w_out, conv_gain, conv_bias, w_conv = call(
        fetch_kernel, [(a.shape, a.dtype) for a in far_args], (),
        far_args=far_args, scratch=[pltpu.SemaphoreType.DMA((len(far_args),))],
    )
    ext = ((2 * edge_slots(width) + (width + 2) * height, channels), BF16)
    raw, queries = call(query_kernel, [ext, ext], (frame, top, bottom, twin, cross, gain, w_query, w_key))
    twin_queries = moved(queries, twin_pairs)
    (partial,) = call(cache_conv_kernel, [((count, out_channels), F32)], (cache, top, bottom, twin, cross, w_conv))
    states = None
    for k in range(0, len(blocks), 4):
        states = fold(states, queries, twin_queries, gain, blocks[k : k + 4])
    other = moved(states[1], twin_pairs)
    hidden, mixed = call(
        functools.partial(finish_kernel, height),
        [((count, channels), BF16), ((count, out_channels), BF16)],
        (
            states[0], other, queries, last, gain, raw, partial, w_value, w_out, conv_gain, conv_bias,
            w_conv,
        ),
        24 << 20,
        far=True,
    )
    hidden = jnp.transpose(hidden.reshape(width, height, channels), (1, 0, 2))
    mixed = jnp.transpose(mixed.reshape(width, height, out_channels), (1, 0, 2))
    return (hidden, mixed)


def solution(mesh):
    in_specs = (
        P(("video", "rows"), "cols", None),
        P(),
        P(),
        P(),
        P(),
        P(),
        P(),
        P(None, ("video", "rows"), "cols", None),
        P(),
        P(),
    )
    out_specs = (P(("video", "rows"), "cols", None), P(("video", "rows"), "cols", None))
    return jax.shard_map(block, mesh=mesh, in_specs=in_specs, out_specs=out_specs, check_vma=False)
```

profile of v0, /device:TPU:0, one launch (start us, length us, event | category | flops | bytes accessed | tf_op | source)
XLA Modules:
  0.0 42.1 jit_solution(9111215942215208500)
XLA Ops:
  0.6 1.2 %shard_map.113 = (bf16[20,8,512]{2,1,0:T(8,128)(2,1)S(1)}, bf16[2,20,8,512]{3,2,1,0:T(8,128)(2,1)S(1)}, f32[1,512]{1,0:T(1,128)S(1)}, bf16[48,512]{1,0:T(8,128)(2,1)S(1)}, bf16[224,512]{1,0:T(8,128)(2,1)S(1)}) custom-call(bf16[20,8,512]{2,1,0:T(8,128)(2,1)} %bitcast.12, bf16[2,20,8,512]{3,2,1,0:T(8,128)(2,1)} %bitcast.11, f32[1,512]{1,0:T(1,128)} %bitcast.13), custom_call_target="tpu_custom_call" | custom-call | tf_op jit(solution)/shard_map/pallas_call | solution.py:24
  1.8 0.6 %collective-permute-start = (bf16[224,512]{1,0:T(8,128)(2,1)S(1)}, bf16[224,512]{1,0:T(8,128)(2,1)S(1)}, u32[]{:S(2)}, u32[]{:S(2)}) collective-permute-start(bf16[224,512]{1,0:T(8,128)(2,1)S(1)} %get-tuple-element.29), channel_id=1, source_target_pairs={{0,1},{1,0},{2,3},{3,2},{4,5},{5,4},{6,7},{7,6},{8,9},{9,8},{10,11... | collective-permute-start | bytes 688136 | tf_op jit(solution)/shard_map/ppermute | solution.py:444
  2.4 1.1 %collective-permute-done.partner_ref = bf16[224,512]{1,0:T(8,128)(2,1)S(1)} collective-permute-done((bf16[224,512]{1,0:T(8,128)(2,1)S(1)}, bf16[224,512]{1,0:T(8,128)(2,1)S(1)}, u32[]{:S(2)}, u32[]{:S(2)}) %collective-permute-start) | collective-permute-done | bytes 229408 | tf_op jit(solution)/shard_map/ppermute | solution.py:444
  3.6 3.0 %collective-permute-start.1 = (bf16[416,512]{1,0:T(8,128)(2,1)S(1)}, bf16[416,512]{1,0:T(8,128)(2,1)S(1)}, u32[]{:S(2)}, u32[]{:S(2)}) collective-permute-start(bf16[416,512]{1,0:T(8,128)(2,1)S(1)} %shard_map.114), channel_id=1, source_target_pairs={{4,8},{9,5},{8,12},{13,9},{12,14},{15,13},{14,10},{11,15},{10,6},{... | collective-permute-start | bytes 1277960 | tf_op jit(solution)/shard_map/ppermute | solution.py:444
  6.5 6.0 %collective-permute-done.1.arrived_ref = bf16[416,512]{1,0:T(8,128)(2,1)S(1)} collective-permute-done((bf16[416,512]{1,0:T(8,128)(2,1)S(1)}, bf16[416,512]{1,0:T(8,128)(2,1)S(1)}, u32[]{:S(2)}, u32[]{:S(2)}) %collective-permute-start.1) | collective-permute-done | bytes 426016 | tf_op jit(solution)/shard_map/ppermute | solution.py:444
  12.6 0.1 shard_map.115
  12.7 2.2 %collective-permute-start.5 = (bf16[320,512]{1,0:T(8,128)(2,1)S(1)}, bf16[320,512]{1,0:T(8,128)(2,1)S(1)}, u32[]{:S(2)}, u32[]{:S(2)}) collective-permute-start(bf16[320,512]{1,0:T(8,128)(2,1)S(1)} %get-tuple-element.39.refs_1_), channel_id=1, source_target_pairs={{4,8},{9,5},{8,12},{13,9},{12,14},{15,13},{14,10},{11,15},{10,6},{... | collective-permute-start | bytes 983048 | tf_op jit(solution)/shard_map/ppermute | solution.py:444
  14.8 0.0 collective-permute-start.2
  14.8 5.0 %collective-permute-done.5.refs_2_ = bf16[320,512]{1,0:T(8,128)(2,1)S(1)} collective-permute-done((bf16[320,512]{1,0:T(8,128)(2,1)S(1)}, bf16[320,512]{1,0:T(8,128)(2,1)S(1)}, u32[]{:S(2)}, u32[]{:S(2)}) %collective-permute-start.5) | collective-permute-done | bytes 327712 | tf_op jit(solution)/shard_map/ppermute | solution.py:444
  19.8 2.1 %collective-permute-start.6 = (bf16[320,512]{1,0:T(8,128)(2,1)S(1)}, bf16[320,512]{1,0:T(8,128)(2,1)S(1)}, u32[]{:S(2)}, u32[]{:S(2)}) collective-permute-start(bf16[320,512]{1,0:T(8,128)(2,1)S(1)} %collective-permute-done.5.refs_2_), channel_id=1, source_target_pairs={{4,8},{9,5},{8,12},{13,9},{12,14},{15,13},{14,10},{11,15},{10,6},{... | collective-permute-start | bytes 983048 | tf_op jit(solution)/shard_map/ppermute | solution.py:444
  21.9 0.0 collective-permute-done.2.theirs_ref
  21.9 0.1 shard_map.116
  22.0 0.7 %collective-permute-start.3 = (bf16[3,16,512]{2,1,0:T(8,128)(2,1)S(1)}, bf16[3,16,512]{2,1,0:T(8,128)(2,1)S(1)}, u32[]{:S(2)}, u32[]{:S(2)}) collective-permute-start(bf16[3,16,512]{2,1,0:T(8,128)(2,1)S(1)} %get-tuple-element.35), channel_id=1, source_target_pairs={{1,2},{2,1},{5,6},{6,5},{9,10},{10,9},{13,14},{14,13},{17,18},{18,... | collective-permute-start | bytes 147464 | tf_op jit(solution)/shard_map/ppermute | solution.py:444
  22.7 3.8 %shard_map.117 = (bf16[512,512]{1,0:T(8,128)(2,1)S(1)}, bf16[512,512]{1,0:T(8,128)(2,1)S(1)}, bf16[512,512]{1,0:T(8,128)(2,1)S(1)}, bf16[512,512]{1,0:T(8,128)(2...) custom-call(bf16[512,512]{1,0:T(8,128)(2,1)} %refs_0_.1, ...), custom_call_target="tpu_custom_call" | custom-call | tf_op jit(solution)/shard_map/pallas_call | solution.py:24
  26.5 0.0 collective-permute-done.3.cross_ref
  26.5 0.6 %shard_map.118 = (bf16[240,512]{1,0:T(8,128)(2,1)S(1)}, bf16[240,512]{1,0:T(8,128)(2,1)S(1)}) custom-call(bf16[20,8,512]{2,1,0:T(8,128)(2,1)S(1)} %get-tuple-element.27.frame_ref.refs_0_, bf16[3,24,512]{2,1,0:T(8,128)(2,1)S(1)} %get-tuple-element.32.top_ref, bf16[3,24,512]{2,1,0:T(8,128)(2,1)S(1)} %get-tuple-element.33.bottom_ref, ...), custom_call_target="tpu_custom_call" | custom-call | tf_op jit(solution)/shard_map/pallas_call | solution.py:24
  27.1 1.3 %collective-permute-start.4 = (bf16[240,512]{1,0:T(8,128)(2,1)S(1)}, bf16[240,512]{1,0:T(8,128)(2,1)S(1)}, u32[]{:S(2)}, u32[]{:S(2)}) collective-permute-start(bf16[240,512]{1,0:T(8,128)(2,1)S(1)} %get-tuple-element.38.own_ref.query_ref), channel_id=1, source_target_pairs={{0,1},{1,0},{2,3},{3,2},{4,5},{5,4},{6,7},{7,6},{8,9},{9,8},{10,11... | collective-permute-start | bytes 737288 | tf_op jit(solution)/shard_map/ppermute | solution.py:444
  28.4 1.1 %collective-permute-done.4.twin_ref = bf16[240,512]{1,0:T(8,128)(2,1)S(1)} collective-permute-done((bf16[240,512]{1,0:T(8,128)(2,1)S(1)}, bf16[240,512]{1,0:T(8,128)(2,1)S(1)}, u32[]{:S(2)}, u32[]{:S(2)}) %collective-permute-start.4) | collective-permute-done | bytes 245792 | tf_op jit(solution)/shard_map/ppermute | solution.py:444
  29.6 0.0 collective-permute-done.6.refs_3_
  29.6 2.0 %shard_map.119 = (f32[240,768]{1,0:T(8,128)S(1)}, f32[240,768]{1,0:T(8,128)S(1)}) custom-call(f32[1,512]{1,0:T(1,128)S(1)} %get-tuple-element.26.gain_ref.key_gain_ref, bf16[240,512]{1,0:T(8,128)(2,1)S(1)} %get-tuple-element.38.own_ref.query_ref, bf16[240,512]{1,0:T(8,128)(2,1)S(1)} %collective-permute-done.4.twin_ref, ...), custom_call_target="tpu_custom_call" | custom-call | tf_op jit(solution)/shard_map/pallas_call | solution.py:24
  31.6 0.4 %collective-permute-start.7 = (f32[240,768]{1,0:T(8,128)S(1)}, f32[240,768]{1,0:T(8,128)S(1)}, u32[]{:S(2)}, u32[]{:S(2)}) collective-permute-start(f32[240,768]{1,0:T(8,128)S(1)} %get-tuple-element.41), channel_id=1, source_target_pairs={{0,1},{1,0},{2,3},{3,2},{4,5},{5,4},{6,7},{7,6},{8,9},{9,8},{10,11... | collective-permute-start | bytes 2211848 | tf_op jit(solution)/shard_map/ppermute | solution.py:444
  32.0 2.0 %collective-permute-start.8 = (bf16[320,512]{1,0:T(8,128)(2,1)S(1)}, bf16[320,512]{1,0:T(8,128)(2,1)S(1)}, u32[]{:S(2)}, u32[]{:S(2)}) collective-permute-start(bf16[320,512]{1,0:T(8,128)(2,1)S(1)} %collective-permute-done.6.refs_3_), channel_id=1, source_target_pairs={{4,8},{9,5},{8,12},{13,9},{12,14},{15,13},{14,10},{11,15},{10,6},{... | collective-permute-start | bytes 983048 | tf_op jit(solution)/shard_map/ppermute | solution.py:444
  34.0 1.2 %shard_map.120.partial_ref = f32[160,256]{1,0:T(8,128)S(1)} custom-call(bf16[2,20,8,512]{3,2,1,0:T(8,128)(2,1)S(1)} %get-tuple-element.28.cache_ref, bf16[3,24,512]{2,1,0:T(8,128)(2,1)S(1)} %get-tuple-element.32.top_ref, bf16[3,24,512]{2,1,0:T(8,128)(2,1)S(1)} %get-tuple-element.33.bottom_ref, bf16[3,16,512]{2,1,0:T(8,128)(2,1)S(1)} %get-tuple-element.34.twin_ref, ...), custom_call_target="tpu_custom_call" | custom-call | tf_op jit(solution)/shard_map/pallas_call | solution.py:24
  35.2 3.9 %collective-permute-done.8.last_ref = bf16[320,512]{1,0:T(8,128)(2,1)S(1)} collective-permute-done((bf16[320,512]{1,0:T(8,128)(2,1)S(1)}, bf16[320,512]{1,0:T(8,128)(2,1)S(1)}, u32[]{:S(2)}, u32[]{:S(2)}) %collective-permute-start.8) | collective-permute-done | bytes 327712 | tf_op jit(solution)/shard_map/ppermute | solution.py:444
  39.1 0.0 collective-permute-done.7.other_ref
  39.1 3.0 %shard_map.121 = (bf16[160,512]{1,0:T(8,128)(2,1)}, bf16[160,256]{1,0:T(8,128)(2,1)}) custom-call(f32[240,768]{1,0:T(8,128)S(1)} %get-tuple-element.40.state_ref, f32[240,768]{1,0:T(8,128)S(1)} %collective-permute-done.7.other_ref, bf16[240,512]{1,0:T(8,128)(2,1)S(1)} %get-tuple-element.38.own_ref.query_ref, ...), custom_call_target="tpu_custom_call" | custom-call | tf_op jit(solution)/shard_map/pallas_call | solution.py:24
  (1 shorter events, 0.0 us)
Async XLA Ops:
  1.8 1.7 %collective-permute-start = (bf16[224,512]{1,0:T(8,128)(2,1)S(1)}, bf16[224,512]{1,0:T(8,128)(2,1)S(1)}, u32[]{:S(2)}, u32[]{:S(2)}) collective-permute-start(bf16[224,512]{1,0:T(8,128)(2,1)S(1)} %get-tuple-element.29), channel_id=1, source_target_pairs={{0,1},{1,0},{2,3},{3,2},{4,5},{5,4},{6,7},{7,6},{8,9},{9,8},{10,11... | collective-permute-start | bytes 688136 | tf_op jit(solution)/shard_map/ppermute | solution.py:444
  3.6 9.0 %collective-permute-start.1 = (bf16[416,512]{1,0:T(8,128)(2,1)S(1)}, bf16[416,512]{1,0:T(8,128)(2,1)S(1)}, u32[]{:S(2)}, u32[]{:S(2)}) collective-permute-start(bf16[416,512]{1,0:T(8,128)(2,1)S(1)} %shard_map.114), channel_id=1, source_target_pairs={{4,8},{9,5},{8,12},{13,9},{12,14},{15,13},{14,10},{11,15},{10,6},{... | collective-permute-start | bytes 1277960 | tf_op jit(solution)/shard_map/ppermute | solution.py:444
  12.7 7.1 %collective-permute-start.5 = (bf16[320,512]{1,0:T(8,128)(2,1)S(1)}, bf16[320,512]{1,0:T(8,128)(2,1)S(1)}, u32[]{:S(2)}, u32[]{:S(2)}) collective-permute-start(bf16[320,512]{1,0:T(8,128)(2,1)S(1)} %get-tuple-element.39.refs_1_), channel_id=1, source_target_pairs={{4,8},{9,5},{8,12},{13,9},{12,14},{15,13},{14,10},{11,15},{10,6},{... | collective-permute-start | bytes 983048 | tf_op jit(solution)/shard_map/ppermute | solution.py:444
  14.8 7.1 %collective-permute-start.2 = (bf16[144,512]{1,0:T(8,128)(2,1)S(1)}, bf16[144,512]{1,0:T(8,128)(2,1)S(1)}, u32[]{:S(2)}, u32[]{:S(2)}) collective-permute-start(bf16[144,512]{1,0:T(8,128)(2,1)S(1)} %get-tuple-element.31.mine_ref), channel_id=1, source_target_pairs={{0,1},{1,0},{2,3},{3,2},{4,5},{5,4},{6,7},{7,6},{8,9},{9,8},{10,11... | collective-permute-start | bytes 442376 | tf_op jit(solution)/shard_map/ppermute | solution.py:444
  19.8 9.8 %collective-permute-start.6 = (bf16[320,512]{1,0:T(8,128)(2,1)S(1)}, bf16[320,512]{1,0:T(8,128)(2,1)S(1)}, u32[]{:S(2)}, u32[]{:S(2)}) collective-permute-start(bf16[320,512]{1,0:T(8,128)(2,1)S(1)} %collective-permute-done.5.refs_2_), channel_id=1, source_target_pairs={{4,8},{9,5},{8,12},{13,9},{12,14},{15,13},{14,10},{11,15},{10,6},{... | collective-permute-start | bytes 983048 | tf_op jit(solution)/shard_map/ppermute | solution.py:444
  22.0 4.5 %collective-permute-start.3 = (bf16[3,16,512]{2,1,0:T(8,128)(2,1)S(1)}, bf16[3,16,512]{2,1,0:T(8,128)(2,1)S(1)}, u32[]{:S(2)}, u32[]{:S(2)}) collective-permute-start(bf16[3,16,512]{2,1,0:T(8,128)(2,1)S(1)} %get-tuple-element.35), channel_id=1, source_target_pairs={{1,2},{2,1},{5,6},{6,5},{9,10},{10,9},{13,14},{14,13},{17,18},{18,... | collective-permute-start | bytes 147464 | tf_op jit(solution)/shard_map/ppermute | solution.py:444
  27.1 2.5 %collective-permute-start.4 = (bf16[240,512]{1,0:T(8,128)(2,1)S(1)}, bf16[240,512]{1,0:T(8,128)(2,1)S(1)}, u32[]{:S(2)}, u32[]{:S(2)}) collective-permute-start(bf16[240,512]{1,0:T(8,128)(2,1)S(1)} %get-tuple-element.38.own_ref.query_ref), channel_id=1, source_target_pairs={{0,1},{1,0},{2,3},{3,2},{4,5},{5,4},{6,7},{7,6},{8,9},{9,8},{10,11... | collective-permute-start | bytes 737288 | tf_op jit(solution)/shard_map/ppermute | solution.py:444
  31.6 7.5 %collective-permute-start.7 = (f32[240,768]{1,0:T(8,128)S(1)}, f32[240,768]{1,0:T(8,128)S(1)}, u32[]{:S(2)}, u32[]{:S(2)}) collective-permute-start(f32[240,768]{1,0:T(8,128)S(1)} %get-tuple-element.41), channel_id=1, source_target_pairs={{0,1},{1,0},{2,3},{3,2},{4,5},{5,4},{6,7},{7,6},{8,9},{9,8},{10,11... | collective-permute-start | bytes 2211848 | tf_op jit(solution)/shard_map/ppermute | solution.py:444
  32.0 7.1 %collective-permute-start.8 = (bf16[320,512]{1,0:T(8,128)(2,1)S(1)}, bf16[320,512]{1,0:T(8,128)(2,1)S(1)}, u32[]{:S(2)}, u32[]{:S(2)}) collective-permute-start(bf16[320,512]{1,0:T(8,128)(2,1)S(1)} %collective-permute-done.6.refs_3_), channel_id=1, source_target_pairs={{4,8},{9,5},{8,12},{13,9},{12,14},{15,13},{14,10},{11,15},{10,6},{... | collective-permute-start | bytes 983048 | tf_op jit(solution)/shard_map/ppermute | solution.py:444
where the time goes:
time: 42.2 us; the launch traced here: 42.1 us
  waiting for transfers between devices  17.1 us (41%)
  starting transfers between devices  12.3 us (29%)
  Pallas kernels  11.9 us (28%)
  between operations  0.7 us (2%)
    ppermute x9, waiting for transfers between devices, moved(): return lax.ppermute(value, AXES, pairs)  17.1 us
    ppermute x9, starting transfers between devices, moved(): return lax.ppermute(value, AXES, pairs)  12.3 us
    pallas_call x9, Pallas kernels, call(): pl.pallas_call(kernel, in_specs=[VM] * len(args) + [pl.BlockSpec(memory_s...  11.9 us
  transfers between devices with their start and end apart: 9, of which 5 were waited for; matrix products, arithmetic and copies ran while one was open for 0% of the time, Pallas kernels for 13%

commit v1 on v0

--- a/solution.py
+++ b/solution.py
@@ -12,6 +12,7 @@
 EPS = 1e-06
 AXES = ("rows", "cols")
 F32 = jnp.float32
+COST = 2_000_000_000
 BF16 = jnp.bfloat16
 VM = pl.BlockSpec(memory_space=pltpu.VMEM)
 
@@ -31,6 +32,7 @@
         ],
         scratch_shapes=scratch,
         compiler_params=pltpu.CompilerParams(vmem_limit_bytes=limit),
+        cost_estimate=pl.CostEstimate(flops=COST, bytes_accessed=4 << 20, transcendentals=0),
     )(*[near(a) for a in args], *[pltpu.with_memory_space_constraint(a, pltpu.HBM) for a in far_args])
 
 
@@ -121,45 +123,40 @@
     return lax.rem(lax.rem(col, 2) + lax.div(col, 2), 2)
 
 
-def pack_swap_kernel(frame_hbm, cache_hbm, gain_hbm, frame_ref, cache_ref, gain_ref, edge_ref, swap_ref, sems):
+def pack_chain_kernel(frame_hbm, cache_hbm, gain_hbm, frame_ref, cache_ref, gain_ref, chain_ref, swap_ref, sems):
     load_tiles(frame_hbm, cache_hbm, gain_hbm, frame_ref, cache_ref, gain_ref, sems)
     width, height, channels = frame_ref.shape
     count, rows = width * height, edge_rows(width)
     up = faces_up()
-    odd = lax.rem(lax.axis_index("cols"), 2)
+    chain_ref[:count] = frame_ref[...].reshape(count, channels)
     swap_ref[:count] = frame_ref[...].reshape(count, channels)
     for t in range(2):
         tile = cache_ref[t].astype(F32)
         first, last = row_edge(tile, 0), row_edge(tile, height - 1)
-        edge_ref[t * rows : (t + 1) * rows] = jnp.where(up == 1, first, last).astype(BF16)
         at = count + t * rows
+        chain_ref[at : at + rows] = jnp.where(up == 1, first, last).astype(BF16)
         swap_ref[at : at + rows] = jnp.where(up == 1, last, first).astype(BF16)
-        at = count + 2 * rows + t * height
-        swap_ref[at : at + height] = jnp.where(odd == 1, tile[0], tile[width - 1]).astype(BF16)
-
-
-def join_edges_kernel(frame_ref, edge_ref, partner_ref, out_ref):
-    width, height, channels = frame_ref.shape
-    count, rows = width * height, edge_ref.shape[0]
-    out_ref[:count] = frame_ref[...].reshape(count, channels)
-    out_ref[count : 2 * count] = partner_ref[:count]
-    out_ref[2 * count : 2 * count + rows] = edge_ref[...]
-    out_ref[2 * count + rows :] = partner_ref[count : count + rows]
-
-
-def split_kernel(height, arrived_ref, chain_ref, edges_ref):
-    count = chain_ref.shape[0] // 2
-    width = count // height
-    rows = edge_rows(width)
+
+
+def cut_kernel(arrived_ref, chain_ref):
+    chain_ref[...] = arrived_ref[: chain_ref.shape[0]]
+
+
+def split_kernel(cache_ref, a_ref, b_ref, edges_ref):
+    _, width, height, _ = cache_ref.shape
+    count, rows = width * height, edge_rows(width)
     up = faces_up()
-    chain_ref[...] = arrived_ref[: 2 * count]
-    for k in range(2):
+    odd = lax.rem(lax.axis_index("cols"), 2)
+    for k, ref in enumerate((a_ref, b_ref)):
         to = k * 3 * rows
-        at = 2 * count + k * 2 * rows
-        edges_ref[to : to + 2 * rows] = arrived_ref[at : at + 2 * rows]
-        tile = arrived_ref[k * count : (k + 1) * count].astype(F32).reshape(width, height, -1)
+        edges_ref[to : to + 2 * rows] = ref[count : count + 2 * rows]
+        tile = ref[:count].astype(F32).reshape(width, height, -1)
         edge = jnp.where(up == 1, row_edge(tile, 0), row_edge(tile, height - 1))
         edges_ref[to + 2 * rows : to + 3 * rows] = edge.astype(BF16)
+    for t in range(2):
+        at = 6 * rows + t * height
+        column = jnp.where(odd == 1, cache_ref[t, 0].astype(F32), cache_ref[t, width - 1].astype(F32))
+        edges_ref[at : at + height] = column.astype(BF16)
 
 
 def sort_edges_kernel(
@@ -192,8 +189,8 @@
             block = partner_ref[:count].astype(F32)
             column = facing(odd == 0, block, lambda c: slice(c * height, (c + 1) * height))
         else:
-            at = count + 2 * rows + t * height
-            column = partner_ref[at : at + height].astype(F32)
+            at = 6 * rows + t * height
+            column = theirs_ref[at : at + height].astype(F32)
         corners = [facing(odd == 0, v, lambda c: slice(c, c + 1)) for v in (twin_top, twin_bottom)]
         twin_ref[t] = jnp.concatenate([column, *corners, fill], axis=0).astype(BF16)
         tile = (frame_ref[...] if t == 2 else cache_ref[t]).astype(F32)
@@ -364,21 +361,8 @@
     return call(functools.partial(fold_kernel, len(blocks), first), [shape, shape], args, 24 << 20)
 
 
-def fetch_kernel(*refs):
-    sems = refs[-1]
-    sources, targets = refs[: len(refs) // 2], refs[len(refs) // 2 : -1]
-    copies = [
-        pltpu.make_async_copy(source, target, sems.at[k])
-        for k, (source, target) in enumerate(zip(sources, targets))
-    ]
-    for copy in copies:
-        copy.start()
-    for copy in copies:
-        copy.wait()
-
-
 def finish_kernel(
-    height, state_ref, other_ref, query_ref, last_ref, key_gain_ref, raw_ref, partial_ref,
+    height, state_ref, other_ref, query_ref, last_a_ref, last_b_ref, key_gain_ref, raw_ref, partial_ref,
     wv_ref, wo_ref, gain_ref, bias_ref, w_ref, hidden_ref, mixed_ref,
 ):
     length, channels = raw_ref.shape
@@ -389,7 +373,7 @@
     has_top, has_bottom = row > 0, row < lax.axis_size("rows") - 1
     has_left, has_right = col > 0, col < lax.axis_size("cols") - 1
 
-    keys = key_rows((last_ref,), key_gain_ref[...])
+    keys = key_rows((last_a_ref, last_b_ref), key_gain_ref[...])
     scores = dot_t(query_ref[...], keys)
     peak_a, peak_b = state_ref[:, channels : channels + 1], other_ref[:, channels : channels + 1]
     peak = jnp.maximum(jnp.maximum(peak_a, peak_b), jnp.max(scores, axis=1, keepdims=True))
@@ -430,12 +414,6 @@
     mixed_ref[...] = result.astype(BF16)
 
 
-def join_kernel(a_ref, b_ref, out_ref):
-    count = b_ref.shape[0]
-    out_ref[:count] = a_ref[...].reshape(b_ref.shape)
-    out_ref[count:] = b_ref[...]
-
-
 def narrow(cols):
     return cols == 4
 
@@ -462,19 +440,20 @@
     far_tiles = (frame_far, cache_far, gain_far)
     edge = ((3, rows, channels), BF16)
     side = ((3, side_slots(height), channels), BF16)
-    pair = ((2 * count, channels), BF16)
+    keys = ((count, channels), BF16)
     sems = [pltpu.SemaphoreType.DMA((3,))]
     hops = (chips - 1) // 2
     if narrow(lax.axis_size("cols")):
-        frame, cache, gain, edges, to_partner = call(
-            pack_swap_kernel,
-            tiles + [((2 * rows, channels), BF16), ((count + 2 * (rows + height), channels), BF16)],
-            (), far_args=far_tiles, scratch=sems,
+        with_row = ((count + 2 * rows, channels), BF16)
+        frame, cache, gain, chain_a, to_partner = call(
+            pack_chain_kernel, tiles + [with_row, with_row], (), far_args=far_tiles, scratch=sems
         )
         partner = moved(to_partner, twin_pairs)
-        (first_hop,) = call(join_edges_kernel, [((2 * count + 4 * rows, channels), BF16)], (frame, edges, partner))
-        arrived = moved(first_hop, ring)
-        chain, mine = call(functools.partial(split_kernel, height), [pair, ((6 * rows, channels), BF16)], (arrived,))
+        arrived_a = moved(chain_a, ring)
+        arrived_b = moved(partner, ring)
+        (chain_a,) = call(cut_kernel, [keys], (arrived_a,))
+        (chain_b,) = call(cut_kernel, [keys], (arrived_b,))
+        (mine,) = call(split_kernel, [((6 * rows + 2 * height, channels), BF16)], (cache, arrived_a, arrived_b))
         theirs = moved(mine, twin_pairs)
         top, bottom, twin, to_cross = call(
             sort_edges_kernel, [edge, edge, side, side], (frame, cache, partner, mine, theirs)
@@ -483,41 +462,41 @@
         frame, cache, gain, first_rows, last_rows = call(
             pack_rows_kernel, tiles + [edge, edge], (), far_args=far_tiles, scratch=sems
         )
-        partner = moved(frame_far.reshape(count, channels), twin_pairs)
-        (chain,) = call(join_kernel, [pair], (frame, partner))
-        chain = moved(chain, ring)
+        chain_a = frame_far.reshape(count, channels)
+        chain_b = moved(chain_a, twin_pairs)
+        chain_a = moved(chain_a, ring)
+        chain_b = moved(chain_b, ring)
         top = moved(last_rows, down)
         bottom = moved(first_rows, up)
         to_twin, to_cross = call(pack_cols_kernel, [side, side], (frame, cache, top, bottom))
         twin = moved(to_twin, twin_pairs)
     cross = moved(to_cross, cross_pairs)
-    blocks = [frame, chain]
+    blocks = [frame, chain_a, chain_b]
     for _ in range(1, hops):
-        chain = moved(chain, ring)
-        blocks.append(chain)
-    last = moved(chain, ring)
+        chain_a = moved(chain_a, ring)
+        chain_b = moved(chain_b, ring)
+        blocks += [chain_a, chain_b]
+    last_a = moved(chain_a, ring)
+    last_b = moved(chain_b, ring)
 
     far_args = (
         w_query, w_key, w_value, w_out, conv_gain.reshape(1, channels),
         conv_bias.reshape(1, out_channels), w_conv,
     )
-    w_query, w_key, w_value, w_out, conv_gain, conv_bias, w_conv = call(
-        fetch_kernel, [(a.shape, a.dtype) for a in far_args], (),
-        far_args=far_args, scratch=[pltpu.SemaphoreType.DMA((len(far_args),))],
-    )
+    w_query, w_key, w_value, w_out, conv_gain, conv_bias, w_conv = far_args
     ext = ((2 * edge_slots(width) + (width + 2) * height, channels), BF16)
     raw, queries = call(query_kernel, [ext, ext], (frame, top, bottom, twin, cross, gain, w_query, w_key))
     twin_queries = moved(queries, twin_pairs)
     (partial,) = call(cache_conv_kernel, [((count, out_channels), F32)], (cache, top, bottom, twin, cross, w_conv))
     states = None
-    for k in range(0, len(blocks), 4):
-        states = fold(states, queries, twin_queries, gain, blocks[k : k + 4])
+    for k in range(0, len(blocks), 7):
+        states = fold(states, queries, twin_queries, gain, blocks[k : k + 7])
     other = moved(states[1], twin_pairs)
     hidden, mixed = call(
         functools.partial(finish_kernel, height),
         [((count, channels), BF16), ((count, out_channels), BF16)],
         (
-            states[0], other, queries, last, gain, raw, partial, w_value, w_out, conv_gain, conv_bias,
+            states[0], other, queries, last_a, last_b, gain, raw, partial, w_value, w_out, conv_gain, conv_bias,
             w_conv,
         ),
         24 << 20,

time: 42.2 us -> 39.4 us (0.934)
  starting transfers between devices: 12.3 us -> 19.2 us
  waiting for transfers between devices: 17.1 us -> 11 us
  Pallas kernels: 11.9 us -> 8.19 us
    ppermute x9 -> x13, starting transfers between devices: 12.3 us -> 19.2 us  [moved(): return lax.ppermute(value, AXES, pairs)]
    ppermute x9 -> x13, waiting for transfers between devices: 17.1 us -> 11 us  [moved(): return lax.ppermute(value, AXES, pairs)]
    pallas_call x9, Pallas kernels: 11.9 us -> 8.19 us  [call(): pl.pallas_call(kernel, in_specs=[VM] * len(args) + [pl.BlockSpec(memory_s...]
  transfers between devices with their start and end apart: 9 -> 13, of which waited for: 5 -> 6; matrix products, arithmetic and copies ran while one was open for 0% -> 0% of each run, Pallas kernels for 13% -> 5%
where the time goes in v1:
time: 39.4 us; the launch traced here: 39.2 us
  starting transfers between devices  19.2 us (49%)
  waiting for transfers between devices  11 us (28%)
  Pallas kernels  8.19 us (21%)
  between operations  0.78 us (2%)
    ppermute x13, starting transfers between devices, moved(): return lax.ppermute(value, AXES, pairs)  19.2 us
    ppermute x13, waiting for transfers between devices, moved(): return lax.ppermute(value, AXES, pairs)  11 us
    pallas_call x9, Pallas kernels, call(): pl.pallas_call(kernel, in_specs=[VM] * len(args) + [pl.BlockSpec(memory_s...  8.19 us
  transfers between devices with their start and end apart: 13, of which 6 were waited for; matrix products, arithmetic and copies ran while one was open for 0% of the time, Pallas kernels for 5%

profile of v1, /device:TPU:0, one launch (start us, length us, event | category | flops | bytes accessed | tf_op | source)
XLA Modules:
  0.0 39.2 jit_solution(1406457352866285893)
XLA Ops:
  0.6 1.2 %shard_map.113 = (bf16[20,8,512]{2,1,0:T(8,128)(2,1)S(1)}, bf16[2,20,8,512]{3,2,1,0:T(8,128)(2,1)S(1)}, f32[1,512]{1,0:T(1,128)S(1)}, bf16[208,512]{1,0:T(8,128)(2,1)S(1)}, bf16[208,512]{1,0:T(8,128)(2,1)S(1)}) custom-call(bf16[20,8,512]{2,1,0:T(8,128)(2,1)} %bitcast.16, bf16[2,20,8,512]{3,2,1,0:T(8,128)(2,1)} %bitcast.15, f32[1,512]{1,0:T(1,128)} %bitcast.19), custom_call_target="tpu_custom_call" | custom-call | flops 2000000000 | bytes 4194304 | tf_op jit(solution)/shard_map/pallas_call | solution.py:25
  1.8 0.6 %collective-permute-start = (bf16[208,512]{1,0:T(8,128)(2,1)S(1)}, bf16[208,512]{1,0:T(8,128)(2,1)S(1)}, u32[]{:S(2)}, u32[]{:S(2)}) collective-permute-start(bf16[208,512]{1,0:T(8,128)(2,1)S(1)} %get-tuple-element.20), channel_id=1, source_target_pairs={{0,1},{1,0},{2,3},{3,2},{4,5},{5,4},{6,7},{7,6},{8,9},{9,8},{10,11... | collective-permute-start | bytes 638984 | tf_op jit(solution)/shard_map/ppermute | solution.py:422
  2.4 2.6 %collective-permute-start.1 = (bf16[208,512]{1,0:T(8,128)(2,1)S(1)}, bf16[208,512]{1,0:T(8,128)(2,1)S(1)}, u32[]{:S(2)}, u32[]{:S(2)}) collective-permute-start(bf16[208,512]{1,0:T(8,128)(2,1)S(1)} %get-tuple-element.21), channel_id=1, source_target_pairs={{4,8},{9,5},{8,12},{13,9},{12,14},{15,13},{14,10},{11,15},{10,6},{... | collective-permute-start | bytes 638984 | tf_op jit(solution)/shard_map/ppermute | solution.py:422
  5.0 0.0 collective-permute-done.partner_ref
  5.0 1.6 %collective-permute-start.2 = (bf16[208,512]{1,0:T(8,128)(2,1)S(1)}, bf16[208,512]{1,0:T(8,128)(2,1)S(1)}, u32[]{:S(2)}, u32[]{:S(2)}) collective-permute-start(bf16[208,512]{1,0:T(8,128)(2,1)S(1)} %collective-permute-done.partner_ref), channel_id=1, source_target_pairs={{4,8},{9,5},{8,12},{13,9},{12,14},{15,13},{14,10},{11,15},{10,6},{... | collective-permute-start | bytes 638984 | tf_op jit(solution)/shard_map/ppermute | solution.py:422
  6.6 2.2 %collective-permute-done.1.a_ref.arrived_ref = bf16[208,512]{1,0:T(8,128)(2,1)S(1)} collective-permute-done((bf16[208,512]{1,0:T(8,128)(2,1)S(1)}, bf16[208,512]{1,0:T(8,128)(2,1)S(1)}, u32[]{:S(2)}, u32[]{:S(2)}) %collective-permute-start.1) | collective-permute-done | bytes 213024 | tf_op jit(solution)/shard_map/ppermute | solution.py:422
  8.8 2.3 %collective-permute-done.2.b_ref.arrived_ref = bf16[208,512]{1,0:T(8,128)(2,1)S(1)} collective-permute-done((bf16[208,512]{1,0:T(8,128)(2,1)S(1)}, bf16[208,512]{1,0:T(8,128)(2,1)S(1)}, u32[]{:S(2)}, u32[]{:S(2)}) %collective-permute-start.2) | collective-permute-done | bytes 213024 | tf_op jit(solution)/shard_map/ppermute | solution.py:422
  11.1 0.1 shard_map.114.mine_ref
  11.2 0.1 collective-permute-start.3
  11.3 2.2 %collective-permute-start.6 = (bf16[160,512]{1,0:T(8,128)(2,1)S(1)}, bf16[160,512]{1,0:T(8,128)(2,1)S(1)}, u32[]{:S(2)}, u32[]{:S(2)}) collective-permute-start(bf16[160,512]{1,0:T(8,128)(2,1)S(1)} %shard_map.117.refs_1_), channel_id=1, source_target_pairs={{4,8},{9,5},{8,12},{13,9},{12,14},{15,13},{14,10},{11,15},{10,6},{... | collective-permute-start | bytes 491528 | tf_op jit(solution)/shard_map/ppermute | solution.py:422
  13.4 0.0 collective-permute-done.3.theirs_ref
  13.4 0.0 copy-start.4
  13.4 0.0 copy-start.5
  13.4 0.1 shard_map.115
  13.6 0.8 %collective-permute-start.4 = (bf16[3,16,512]{2,1,0:T(8,128)(2,1)S(1)}, bf16[3,16,512]{2,1,0:T(8,128)(2,1)S(1)}, u32[]{:S(2)}, u32[]{:S(2)}) collective-permute-start(bf16[3,16,512]{2,1,0:T(8,128)(2,1)S(1)} %get-tuple-element.25), channel_id=1, source_target_pairs={{1,2},{2,1},{5,6},{6,5},{9,10},{10,9},{13,14},{14,13},{17,18},{18,... | collective-permute-start | bytes 147464 | tf_op jit(solution)/shard_map/ppermute | solution.py:422
  14.4 1.6 %collective-permute-start.7 = (bf16[160,512]{1,0:T(8,128)(2,1)S(1)}, bf16[160,512]{1,0:T(8,128)(2,1)S(1)}, u32[]{:S(2)}, u32[]{:S(2)}) collective-permute-start(bf16[160,512]{1,0:T(8,128)(2,1)S(1)} %shard_map.118.refs_2_), channel_id=1, source_target_pairs={{4,8},{9,5},{8,12},{13,9},{12,14},{15,13},{14,10},{11,15},{10,6},{... | collective-permute-start | bytes 491528 | tf_op jit(solution)/shard_map/ppermute | solution.py:422
  16.0 0.0 collective-permute-done.4.cross_ref
  16.0 0.0 slice-start
  16.0 0.0 copy-done.4
  16.0 0.0 copy-done.5
  16.0 0.0 slice-start.1
  16.0 0.6 %shard_map.116 = (bf16[240,512]{1,0:T(8,128)(2,1)S(1)}, bf16[240,512]{1,0:T(8,128)(2,1)S(1)}) custom-call(bf16[20,8,512]{2,1,0:T(8,128)(2,1)S(1)} %get-tuple-element.18.frame_ref.refs_0_, bf16[3,24,512]{2,1,0:T(8,128)(2,1)S(1)} %get-tuple-element.22.top_ref, bf16[3,24,512]{2,1,0:T(8,128)(2,1)S(1)} %get-tuple-element.23.bottom_ref, ...), custom_call_target="tpu_custom_call" | custom-call | flops 2000000000 | bytes 4194304 | tf_op jit(solution)/shard_map/pallas_call | solution.py:25
  16.6 0.0 copy-start
  16.6 0.0 copy-start.1
  16.7 0.0 copy-start.2
  16.7 0.0 copy-start.3
  16.7 3.3 %collective-permute-start.5 = (bf16[240,512]{1,0:T(8,128)(2,1)S(1)}, bf16[240,512]{1,0:T(8,128)(2,1)S(1)}, u32[]{:S(2)}, u32[]{:S(2)}) collective-permute-start(bf16[240,512]{1,0:T(8,128)(2,1)S(1)} %get-tuple-element.26.own_ref.query_ref), channel_id=1, source_target_pairs={{0,1},{1,0},{2,3},{3,2},{4,5},{5,4},{6,7},{7,6},{8,9},{9,8},{10,11... | collective-permute-start | bytes 737288 | tf_op jit(solution)/shard_map/ppermute | solution.py:422
  20.0 0.0 collective-permute-done.6.refs_3_
  20.0 1.6 %collective-permute-start.8 = (bf16[160,512]{1,0:T(8,128)(2,1)S(1)}, bf16[160,512]{1,0:T(8,128)(2,1)S(1)}, u32[]{:S(2)}, u32[]{:S(2)}) collective-permute-start(bf16[160,512]{1,0:T(8,128)(2,1)S(1)} %collective-permute-done.6.refs_3_), channel_id=1, source_target_pairs={{4,8},{9,5},{8,12},{13,9},{12,14},{15,13},{14,10},{11,15},{10,6},{... | collective-permute-start | bytes 491528 | tf_op jit(solution)/shard_map/ppermute | solution.py:422
  21.6 0.0 collective-permute-done.7.refs_4_
  21.6 1.6 %collective-permute-start.9 = (bf16[160,512]{1,0:T(8,128)(2,1)S(1)}, bf16[160,512]{1,0:T(8,128)(2,1)S(1)}, u32[]{:S(2)}, u32[]{:S(2)}) collective-permute-start(bf16[160,512]{1,0:T(8,128)(2,1)S(1)} %collective-permute-done.7.refs_4_), channel_id=1, source_target_pairs={{4,8},{9,5},{8,12},{13,9},{12,14},{15,13},{14,10},{11,15},{10,6},{... | collective-permute-start | bytes 491528 | tf_op jit(solution)/shard_map/ppermute | solution.py:422
  23.2 2.1 %collective-permute-done.8.refs_5_ = bf16[160,512]{1,0:T(8,128)(2,1)S(1)} collective-permute-done((bf16[160,512]{1,0:T(8,128)(2,1)S(1)}, bf16[160,512]{1,0:T(8,128)(2,1)S(1)}, u32[]{:S(2)}, u32[]{:S(2)}) %collective-permute-start.8) | collective-permute-done | bytes 163872 | tf_op jit(solution)/shard_map/ppermute | solution.py:422
  25.3 1.8 %collective-permute-done.9.refs_6_ = bf16[160,512]{1,0:T(8,128)(2,1)S(1)} collective-permute-done((bf16[160,512]{1,0:T(8,128)(2,1)S(1)}, bf16[160,512]{1,0:T(8,128)(2,1)S(1)}, u32[]{:S(2)}, u32[]{:S(2)}) %collective-permute-start.9) | collective-permute-done | bytes 163872 | tf_op jit(solution)/shard_map/ppermute | solution.py:422
  27.0 0.0 collective-permute-done.5.twin_ref
  27.0 2.0 %shard_map.119 = (f32[240,768]{1,0:T(8,128)S(1)}, f32[240,768]{1,0:T(8,128)S(1)}) custom-call(f32[1,512]{1,0:T(1,128)S(1)} %get-tuple-element.17.gain_ref.key_gain_ref, bf16[240,512]{1,0:T(8,128)(2,1)S(1)} %get-tuple-element.26.own_ref.query_ref, bf16[240,512]{1,0:T(8,128)(2,1)S(1)} %collective-permute-done.5.twin_ref, ...), custom_call_target="tpu_custom_call" | custom-call | flops 2000000000 | bytes 4194304 | tf_op jit(solution)/shard_map/pallas_call | solution.py:25
  29.0 0.1 collective-permute-start.10
  29.1 1.7 %collective-permute-start.11 = (bf16[160,512]{1,0:T(8,128)(2,1)S(1)}, bf16[160,512]{1,0:T(8,128)(2,1)S(1)}, u32[]{:S(2)}, u32[]{:S(2)}) collective-permute-start(bf16[160,512]{1,0:T(8,128)(2,1)S(1)} %collective-permute-done.8.refs_5_), channel_id=1, source_target_pairs={{4,8},{9,5},{8,12},{13,9},{12,14},{15,13},{14,10},{11,15},{10,6},{... | collective-permute-start | bytes 491528 | tf_op jit(solution)/shard_map/ppermute | solution.py:422
  30.8 1.6 %collective-permute-start.12 = (bf16[160,512]{1,0:T(8,128)(2,1)S(1)}, bf16[160,512]{1,0:T(8,128)(2,1)S(1)}, u32[]{:S(2)}, u32[]{:S(2)}) collective-permute-start(bf16[160,512]{1,0:T(8,128)(2,1)S(1)} %collective-permute-done.9.refs_6_), channel_id=1, source_target_pairs={{4,8},{9,5},{8,12},{13,9},{12,14},{15,13},{14,10},{11,15},{10,6},{... | collective-permute-start | bytes 491528 | tf_op jit(solution)/shard_map/ppermute | solution.py:422
  32.3 0.0 slice-done
  32.3 0.0 slice-done.1
  32.3 1.2 %shard_map.120.partial_ref = f32[160,256]{1,0:T(8,128)S(1)} custom-call(bf16[2,20,8,512]{3,2,1,0:T(8,128)(2,1)S(1)} %get-tuple-element.19.cache_ref, bf16[3,24,512]{2,1,0:T(8,128)(2,1)S(1)} %get-tuple-element.22.top_ref, bf16[3,24,512]{2,1,0:T(8,128)(2,1)S(1)} %get-tuple-element.23.bottom_ref, bf16[3,16,512]{2,1,0:T(8,128)(2,1)S(1)} %get-tuple-element.24.twin_ref, ...), custom_call_target="tpu_custom_call" | custom-call | flops 2000000000 | bytes 4194304 | tf_op jit(solution)/shard_map/pallas_call | solution.py:25
  33.5 0.9 %collective-permute-done.11.last_a_ref = bf16[160,512]{1,0:T(8,128)(2,1)S(1)} collective-permute-done((bf16[160,512]{1,0:T(8,128)(2,1)S(1)}, bf16[160,512]{1,0:T(8,128)(2,1)S(1)}, u32[]{:S(2)}, u32[]{:S(2)}) %collective-permute-start.11) | collective-permute-done | bytes 163872 | tf_op jit(solution)/shard_map/ppermute | solution.py:422
  34.5 1.8 %collective-permute-done.12.last_b_ref = bf16[160,512]{1,0:T(8,128)(2,1)S(1)} collective-permute-done((bf16[160,512]{1,0:T(8,128)(2,1)S(1)}, bf16[160,512]{1,0:T(8,128)(2,1)S(1)}, u32[]{:S(2)}, u32[]{:S(2)}) %collective-permute-start.12) | collective-permute-done | bytes 163872 | tf_op jit(solution)/shard_map/ppermute | solution.py:422
  36.2 0.0 collective-permute-done.10.other_ref
  36.2 0.0 copy-done
  36.2 0.0 copy-done.1
  36.2 0.0 copy-done.2
  36.2 0.0 copy-done.3
  36.3 3.0 %shard_map.121 = (bf16[160,512]{1,0:T(8,128)(2,1)}, bf16[160,256]{1,0:T(8,128)(2,1)}) custom-call(f32[240,768]{1,0:T(8,128)S(1)} %get-tuple-element.27.state_ref, f32[240,768]{1,0:T(8,128)S(1)} %collective-permute-done.10.other_ref, bf16[240,512]{1,0:T(8,128)(2,1)S(1)} %get-tuple-element.26.own_ref.query_ref, ...), custom_call_target="tpu_custom_call" | custom-call | flops 2000000000 | bytes 4194304 | tf_op jit(solution)/shard_map/pallas_call | solution.py:25
  (3 shorter events, 0.0 us)
Async XLA Ops:
  1.8 3.2 %collective-permute-start = (bf16[208,512]{1,0:T(8,128)(2,1)S(1)}, bf16[208,512]{1,0:T(8,128)(2,1)S(1)}, u32[]{:S(2)}, u32[]{:S(2)}) collective-permute-start(bf16[208,512]{1,0:T(8,128)(2,1)S(1)} %get-tuple-element.20), channel_id=1, source_target_pairs={{0,1},{1,0},{2,3},{3,2},{4,5},{5,4},{6,7},{7,6},{8,9},{9,8},{10,11... | collective-permute-start | bytes 638984 | tf_op jit(solution)/shard_map/ppermute | solution.py:422
  2.4 6.4 %collective-permute-start.1 = (bf16[208,512]{1,0:T(8,128)(2,1)S(1)}, bf16[208,512]{1,0:T(8,128)(2,1)S(1)}, u32[]{:S(2)}, u32[]{:S(2)}) collective-permute-start(bf16[208,512]{1,0:T(8,128)(2,1)S(1)} %get-tuple-element.21), channel_id=1, source_target_pairs={{4,8},{9,5},{8,12},{13,9},{12,14},{15,13},{14,10},{11,15},{10,6},{... | collective-permute-start | bytes 638984 | tf_op jit(solution)/shard_map/ppermute | solution.py:422
  5.0 6.0 %collective-permute-start.2 = (bf16[208,512]{1,0:T(8,128)(2,1)S(1)}, bf16[208,512]{1,0:T(8,128)(2,1)S(1)}, u32[]{:S(2)}, u32[]{:S(2)}) collective-permute-start(bf16[208,512]{1,0:T(8,128)(2,1)S(1)} %collective-permute-done.partner_ref), channel_id=1, source_target_pairs={{4,8},{9,5},{8,12},{13,9},{12,14},{15,13},{14,10},{11,15},{10,6},{... | collective-permute-start | bytes 638984 | tf_op jit(solution)/shard_map/ppermute | solution.py:422
  11.2 2.3 %collective-permute-start.3 = (bf16[160,512]{1,0:T(8,128)(2,1)S(1)}, bf16[160,512]{1,0:T(8,128)(2,1)S(1)}, u32[]{:S(2)}, u32[]{:S(2)}) collective-permute-start(bf16[160,512]{1,0:T(8,128)(2,1)S(1)} %shard_map.114.mine_ref), channel_id=1, source_target_pairs={{0,1},{1,0},{2,3},{3,2},{4,5},{5,4},{6,7},{7,6},{8,9},{9,8},{10,11... | collective-permute-start | bytes 491528 | tf_op jit(solution)/shard_map/ppermute | solution.py:422
  11.3 8.7 %collective-permute-start.6 = (bf16[160,512]{1,0:T(8,128)(2,1)S(1)}, bf16[160,512]{1,0:T(8,128)(2,1)S(1)}, u32[]{:S(2)}, u32[]{:S(2)}) collective-permute-start(bf16[160,512]{1,0:T(8,128)(2,1)S(1)} %shard_map.117.refs_1_), channel_id=1, source_target_pairs={{4,8},{9,5},{8,12},{13,9},{12,14},{15,13},{14,10},{11,15},{10,6},{... | collective-permute-start | bytes 491528 | tf_op jit(solution)/shard_map/ppermute | solution.py:422
  13.4 2.6 %copy-start.4 = (bf16[512,512]{1,0:T(8,128)(2,1)S(1)}, bf16[512,512]{1,0:T(8,128)(2,1)}, u32[]{:S(2)}) copy-start(bf16[512,512]{1,0:T(8,128)(2,1)} %wq_ref.1) | copy-start | bytes 1572868
  13.4 2.6 %copy-start.5 = (bf16[512,512]{1,0:T(8,128)(2,1)S(1)}, bf16[512,512]{1,0:T(8,128)(2,1)}, u32[]{:S(2)}) copy-start(bf16[512,512]{1,0:T(8,128)(2,1)} %wk_ref.1) | copy-start | bytes 1572868
  13.6 2.5 %collective-permute-start.4 = (bf16[3,16,512]{2,1,0:T(8,128)(2,1)S(1)}, bf16[3,16,512]{2,1,0:T(8,128)(2,1)S(1)}, u32[]{:S(2)}, u32[]{:S(2)}) collective-permute-start(bf16[3,16,512]{2,1,0:T(8,128)(2,1)S(1)} %get-tuple-element.25), channel_id=1, source_target_pairs={{1,2},{2,1},{5,6},{6,5},{9,10},{10,9},{13,14},{14,13},{17,18},{18,... | collective-permute-start | bytes 147464 | tf_op jit(solution)/shard_map/ppermute | solution.py:422
  14.4 7.2 %collective-permute-start.7 = (bf16[160,512]{1,0:T(8,128)(2,1)S(1)}, bf16[160,512]{1,0:T(8,128)(2,1)S(1)}, u32[]{:S(2)}, u32[]{:S(2)}) collective-permute-start(bf16[160,512]{1,0:T(8,128)(2,1)S(1)} %shard_map.118.refs_2_), channel_id=1, source_target_pairs={{4,8},{9,5},{8,12},{13,9},{12,14},{15,13},{14,10},{11,15},{10,6},{... | collective-permute-start | bytes 491528 | tf_op jit(solution)/shard_map/ppermute | solution.py:422
  16.0 16.3 %slice-start = ((s8[7077888]{0:T(1024)(128)(4,1)}), s8[4194304]{0:T(1024)(128)(4,1)S(1)}, s32[]{:S(2)}) async-start(s8[7077888]{0:T(1024)(128)(4,1)} %bitcast.11), calls=%async_computation | async-start | bytes 8388608
  16.0 16.3 %slice-start.1 = ((s8[7077888]{0:T(1024)(128)(4,1)}), s8[2883584]{0:T(1024)(128)(4,1)S(1)}, s32[]{:S(2)}) async-start(s8[7077888]{0:T(1024)(128)(4,1)} %bitcast.11), calls=%async_computation.1 | async-start | bytes 5767168
  16.6 19.6 %copy-start = (bf16[512,512]{1,0:T(8,128)(2,1)S(1)}, bf16[512,512]{1,0:T(8,128)(2,1)}, u32[]{:S(2)}) copy-start(bf16[512,512]{1,0:T(8,128)(2,1)} %wv_ref.1) | copy-start | bytes 1572868
  16.6 19.6 %copy-start.1 = (bf16[512,512]{1,0:T(8,128)(2,1)S(1)}, bf16[512,512]{1,0:T(8,128)(2,1)}, u32[]{:S(2)}) copy-start(bf16[512,512]{1,0:T(8,128)(2,1)} %wo_ref.1) | copy-start | bytes 1572868
  16.7 19.6 %copy-start.2 = (f32[512]{0:T(512)S(1)}, f32[512]{0:T(512)}, u32[]{:S(2)}) copy-start(f32[512]{0:T(512)} %param.16) | copy-start | bytes 6148
  16.7 19.6 %copy-start.3 = (f32[256]{0:T(256)S(1)}, f32[256]{0:T(256)}, u32[]{:S(2)}) copy-start(f32[256]{0:T(256)} %param.19) | copy-start | bytes 3076
  16.7 10.4 %collective-permute-start.5 = (bf16[240,512]{1,0:T(8,128)(2,1)S(1)}, bf16[240,512]{1,0:T(8,128)(2,1)S(1)}, u32[]{:S(2)}, u32[]{:S(2)}) collective-permute-start(bf16[240,512]{1,0:T(8,128)(2,1)S(1)} %get-tuple-element.26.own_ref.query_ref), channel_id=1, source_target_pairs={{0,1},{1,0},{2,3},{3,2},{4,5},{5,4},{6,7},{7,6},{8,9},{9,8},{10,11... | collective-permute-start | bytes 737288 | tf_op jit(solution)/shard_map/ppermute | solution.py:422
  20.0 5.3 %collective-permute-start.8 = (bf16[160,512]{1,0:T(8,128)(2,1)S(1)}, bf16[160,512]{1,0:T(8,128)(2,1)S(1)}, u32[]{:S(2)}, u32[]{:S(2)}) collective-permute-start(bf16[160,512]{1,0:T(8,128)(2,1)S(1)} %collective-permute-done.6.refs_3_), channel_id=1, source_target_pairs={{4,8},{9,5},{8,12},{13,9},{12,14},{15,13},{14,10},{11,15},{10,6},{... | collective-permute-start | bytes 491528 | tf_op jit(solution)/shard_map/ppermute | solution.py:422
  21.6 5.5 %collective-permute-start.9 = (bf16[160,512]{1,0:T(8,128)(2,1)S(1)}, bf16[160,512]{1,0:T(8,128)(2,1)S(1)}, u32[]{:S(2)}, u32[]{:S(2)}) collective-permute-start(bf16[160,512]{1,0:T(8,128)(2,1)S(1)} %collective-permute-done.7.refs_4_), channel_id=1, source_target_pairs={{4,8},{9,5},{8,12},{13,9},{12,14},{15,13},{14,10},{11,15},{10,6},{... | collective-permute-start | bytes 491528 | tf_op jit(solution)/shard_map/ppermute | solution.py:422
  29.0 7.2 %collective-permute-start.10 = (f32[240,768]{1,0:T(8,128)S(1)}, f32[240,768]{1,0:T(8,128)S(1)}, u32[]{:S(2)}, u32[]{:S(2)}) collective-permute-start(f32[240,768]{1,0:T(8,128)S(1)} %get-tuple-element.28), channel_id=1, source_target_pairs={{0,1},{1,0},{2,3},{3,2},{4,5},{5,4},{6,7},{7,6},{8,9},{9,8},{10,11... | collective-permute-start | bytes 2211848 | tf_op jit(solution)/shard_map/ppermute | solution.py:422
  29.1 5.4 %collective-permute-start.11 = (bf16[160,512]{1,0:T(8,128)(2,1)S(1)}, bf16[160,512]{1,0:T(8,128)(2,1)S(1)}, u32[]{:S(2)}, u32[]{:S(2)}) collective-permute-start(bf16[160,512]{1,0:T(8,128)(2,1)S(1)} %collective-permute-done.8.refs_5_), channel_id=1, source_target_pairs={{4,8},{9,5},{8,12},{13,9},{12,14},{15,13},{14,10},{11,15},{10,6},{... | collective-permute-start | bytes 491528 | tf_op jit(solution)/shard_map/ppermute | solution.py:422
  30.8 5.5 %collective-permute-start.12 = (bf16[160,512]{1,0:T(8,128)(2,1)S(1)}, bf16[160,512]{1,0:T(8,128)(2,1)S(1)}, u32[]{:S(2)}, u32[]{:S(2)}) collective-permute-start(bf16[160,512]{1,0:T(8,128)(2,1)S(1)} %collective-permute-done.9.refs_6_), channel_id=1, source_target_pairs={{4,8},{9,5},{8,12},{13,9},{12,14},{15,13},{14,10},{11,15},{10,6},{... | collective-permute-start | bytes 491528 | tf_op jit(solution)/shard_map/ppermute | solution.py:422
